TPU v7x, 512 devices: a whole 4x4x16 slice. The times are simulated.
512 devices in a mesh: box: 64 (over y, z), row: 8 (over x, core).
Axes of the slice: x: 4, y: 4, z: 16, core: 2. Of those that a mesh axis runs over, the one named last changes fastest.
Arguments:
- rhs: float32 [512, 64, 320], P('box'), may hold values from -6 to 6
- skel1: int32 [512, 192], P('box'), may hold values from 0 to 319, as said below
- red1: int32 [512, 128], P('box'), may hold values from 0 to 319, as said below
- interp1: bfloat16 [512, 128, 192], P('box', None, 'row'), may hold values from -0.5 to 0.5
- inv1: bfloat16 [512, 128, 128], P('box', None, 'row'), may hold values from -0.5 to 0.5
- couple1: bfloat16 [512, 8, 128, 192], P('box', None, None, 'row'), may hold values from -0.5 to 0.5
- near1: int32 [512, 8], P('box'), may hold values from -1 to 511, as said below
- skel2: int32 [64, 384], P('box'), may hold values from 0 to 1535, as said below
- red2: int32 [64, 1152], P('box'), may hold values from 0 to 1535, as said below
- interp2: bfloat16 [64, 1152, 384], P('box', None, 'row'), may hold values from -0.1875 to 0.1875
- inv2: bfloat16 [64, 1152, 1152], P('box', None, 'row'), may hold values from -0.1875 to 0.1875
- panel2: bfloat16 [64, 2, 1152, 384], P('box', None, None, 'row'), may hold values from -0.1875 to 0.1875
- near2: int32 [64, 2], P('box'), may hold values from -1 to 63, as said below
Outputs:
- red_one: float32 [512, 64, 128], P('box', None, 'row')
- red_two: float32 [64, 64, 1152], P('box', None, 'row')
- skel_two: float32 [64, 64, 384], P('box', None, 'row')
Inputs may be any that keep to these rules, and one draw needn't show every extreme that they name: For each leaf box, skel1 and red1 together hold every number below 320 exactly once. `red1`: see skel1. For each parent box, skel2 and red2 together hold every number below 1536 exactly once. `red2`: see skel2. `near1`: an entry of box b is -1 or another leaf box c with |c // 8 - b // 8| <= 2; a box may be named twice. `near2`: slot 0 of parent q is q - 1 or -1, slot 1 is q + 1 or -1.
All inputs are finite; a program needn't handle non-finite values.
Results may differ from a plain program's by a relative error of at most 0.0046.
Values may be sent and summed in bfloat16 or wider, within the bound.
A program may use at most 64 MiB of HBM per device.

v0:
```python
import jax
import jax.numpy as jnp
from jax import lax
from jax.sharding import PartitionSpec as P


def shifted(block, axis, distance):
    devices = range(lax.axis_size(axis))
    route = [(i - distance, i) for i in devices if i - distance in devices]
    return lax.ppermute(block, axis, route)


def pick(values, index):
    return jax.vmap(lambda block, where: block[:, where])(values, index)


def route(updates, near, reach):
    groups = updates.shape[0]
    anchor = lax.axis_index("box")
    valid = near >= 0
    target = jnp.where(valid, near, 0)
    offset = target // groups - anchor
    slot = target % groups
    spots = jnp.arange(2 * reach + 1, dtype=jnp.int32) - reach
    places = jnp.arange(groups, dtype=jnp.int32)
    onehot = (
        valid[:, :, None, None]
        & (offset[:, :, None, None] == spots[None, None, :, None])
        & (slot[:, :, None, None] == places[None, None, None, :])
    ).astype(jnp.float32)
    outgoing = jnp.einsum("gnos,gnkc->oskc", onehot, updates, precision=lax.Precision.HIGHEST)
    total = outgoing[reach]
    for section in range(1, reach + 1):
        for sign in (1, -1):
            moved = shifted(outgoing[reach + sign * section], "box", sign * section)
            total = total + moved
    return total


def shards(
    rhs, skel1, red1, interp1, inv1, couple1, near1, skel2, red2, interp2, inv2, panel2, near2
):
    row_index = lax.axis_index("row")
    s1_block = interp1.shape[2]
    s2_block = interp2.shape[2]
    xr1 = pick(rhs, red1).astype(jnp.bfloat16)
    own_skel1 = lax.dynamic_slice_in_dim(skel1, row_index * s1_block, s1_block, 1)
    ys1 = pick(rhs, own_skel1) - jnp.einsum(
        "bkr,brs->bks", xr1, interp1, preferred_element_type=jnp.float32
    )
    red_one = jnp.einsum("bkr,brq->bkq", xr1, inv1, preferred_element_type=jnp.float32)
    w_one = red_one.astype(jnp.bfloat16)
    u_one = jnp.einsum(
        "bkr,bjrs->bjks",
        lax.all_gather(w_one, "row", axis=2, tiled=True),
        couple1,
        preferred_element_type=jnp.float32,
    )
    routed_one = route(u_one, near1, 2)
    gathered = lax.all_gather(ys1 + routed_one, "row", axis=2, tiled=True)
    children, columns, skeletons = gathered.shape
    parent = jnp.transpose(gathered, (1, 0, 2)).reshape(1, columns, children * skeletons)
    xr2 = pick(parent, red2).astype(jnp.bfloat16)
    own_skel2 = lax.dynamic_slice_in_dim(skel2, row_index * s2_block, s2_block, 1)
    ys2 = pick(parent, own_skel2) - jnp.einsum(
        "pkr,prs->pks", xr2, interp2, preferred_element_type=jnp.float32
    )
    red_two = jnp.einsum("pkr,prq->pkq", xr2, inv2, preferred_element_type=jnp.float32)
    u_two = jnp.einsum("kr,jrs->jks", xr2[0], panel2[0], preferred_element_type=jnp.float32)[None]
    routed_two = route(u_two, near2, 1)
    return (red_one, red_two, ys2 + routed_two)


def solution(mesh):
    return jax.shard_map(
        shards,
        mesh=mesh,
        in_specs=(
            P("box", None, None),
            P("box", None),
            P("box", None),
            P("box", None, "row"),
            P("box", None, "row"),
            P("box", None, None, "row"),
            P("box", None),
            P("box", None),
            P("box", None),
            P("box", None, "row"),
            P("box", None, "row"),
            P("box", None, None, "row"),
            P("box", None),
        ),
        out_specs=(P("box", None, "row"), P("box", None, "row"), P("box", None, "row")),
        check_vma=False,
    )
```

profile of v0, /device:TPU:24, one launch (start us, length us, event | category | flops | bytes accessed | tf_op | source)
XLA Modules:
  0.0 88.1 jit_solution(9671510003143778982)
XLA Ops:
  0.7 0.7 broadcast_compare_fusion
  1.4 0.7 fusion.35
  2.1 0.7 fusion.30
  2.8 1.5 %copy.28 = f32[8,64,320]{1,2,0:T(8,128)S(1)} copy(f32[8,64,320]{2,1,0:T(8,128)} %param.13) | data formatting | bytes 1310720 | tf_op args[0]
  4.4 6.9 %gather_fusion = bf16[1024,64]{1,0:T(8,128)(2,1)S(1)} fusion(f32[8,64,320]{1,2,0:T(8,128)S(1)} %copy.28, s32[1024]{0:T(1024)S(1)} %fusion.35), kind=kCustom, calls=%fused_computation | custom fusion | bytes 270336 | tf_op jit(solution)/shard_map/vmap()/gather | solution.py:14
  11.3 0.8 fusion.56
  12.1 13.2 %all_gather.6 = bf16[8,64,128]{1,2,0:T(8,128)(2,1)S(1)} all-gather(bf16[8,64,16]{1,2,0:T(8,128)(2,1)S(1)} %get-tuple-element.13), channel_id=1, replica_groups=mesh['box'=64,'row'=8] {'row'}, dimensions={2}, use_global_device_ids=true | all-gather | bytes 147456 | tf_op jit(solution)/shard_map/all_gather | solution.py:55
  25.3 0.3 fusion.6
  25.6 0.9 %convolution_bitcast_fusion = f32[5,8,64,24]{2,1,3,0:T(8,128)S(1)} fusion(f32[8,64,8,24]{1,3,2,0:T(8,128)S(1)} %fusion.6, pred[8,8,8]{1,2,0:T(8,128)(4,1)S(1)} %iota_compare_fusion, pred[8,8,5]{1,0,2:T(8,128)(4,1)S(1)} %compare_and_fusion), kind=kOutput, calls=%fused_computation.4 | convolution fusion | flops 47188480 | bytes 639808 | tf_op jit(solution)/shard_map/gnos,gnkc->oskc/dot_general | solution.py:31
  26.6 12.0 %collective-permute-start.3 = (f32[8,64,24]{1,2,0:T(8,128)S(1)}, f32[8,64,24]{1,2,0:T(8,128)S(1)}, u32[]{:S(2)}, u32[]{:S(2)}) collective-permute-start(f32[8,64,24]{1,2,0:T(8,128)S(1)} %bitcast.123), channel_id=1, source_target_pairs={{16,0},{24,8},{32,16},{40,24},{48,32},{56,40},{64,48},{72,56},{80,... | collective-permute-start | bytes 147464 | tf_op jit(solution)/shard_map/ppermute | solution.py:10
  38.7 2.9 %collective-permute-start = (f32[8,64,24]{1,2,0:T(8,128)S(1)}, f32[8,64,24]{1,2,0:T(8,128)S(1)}, u32[]{:S(2)}, u32[]{:S(2)}) collective-permute-start(f32[8,64,24]{1,2,0:T(8,128)S(1)} %bitcast.124), channel_id=1, source_target_pairs={{0,8},{8,16},{16,24},{24,32},{32,40},{40,48},{48,56},{56,64},{64,7... | collective-permute-start | bytes 147464 | tf_op jit(solution)/shard_map/ppermute | solution.py:10
  41.6 5.0 %collective-permute-start.1 = (f32[8,64,24]{1,2,0:T(8,128)S(1)}, f32[8,64,24]{1,2,0:T(8,128)S(1)}, u32[]{:S(2)}, u32[]{:S(2)}) collective-permute-start(f32[8,64,24]{1,2,0:T(8,128)S(1)} %bitcast.125), channel_id=1, source_target_pairs={{8,0},{16,8},{24,16},{32,24},{40,32},{48,40},{56,48},{64,56},{72,6... | collective-permute-start | bytes 147464 | tf_op jit(solution)/shard_map/ppermute | solution.py:10
  46.7 2.1 %collective-permute-start.2 = (f32[8,64,24]{1,2,0:T(8,128)S(1)}, f32[8,64,24]{1,2,0:T(8,128)S(1)}, u32[]{:S(2)}, u32[]{:S(2)}) collective-permute-start(f32[8,64,24]{1,2,0:T(8,128)S(1)} %bitcast.126), channel_id=1, source_target_pairs={{0,16},{8,24},{16,32},{24,40},{32,48},{40,56},{48,64},{56,72},{64,... | collective-permute-start | bytes 147464 | tf_op jit(solution)/shard_map/ppermute | solution.py:10
  48.8 0.8 fusion.48
  49.9 2.2 %gather_fusion.1 = f32[192,64]{1,0:T(8,128)S(1)} fusion(f32[8,64,320]{1,2,0:T(8,128)S(1)} %copy.28, s32[192]{0:T(256)S(1)} %reshape.177), kind=kCustom, calls=%fused_computation.1 | custom fusion | bytes 99840 | tf_op jit(solution)/shard_map/vmap()/gather | solution.py:14
  52.1 5.2 %collective-permute-done.2 = f32[8,64,24]{1,2,0:T(8,128)S(1)} collective-permute-done((f32[8,64,24]{1,2,0:T(8,128)S(1)}, f32[8,64,24]{1,2,0:T(8,128)S(1)}, u32[]{:S(2)}, u32[]{:S(2)}) %collective-permute-start.2) | collective-permute-done | bytes 49184 | tf_op jit(solution)/shard_map/ppermute | solution.py:10
  57.5 13.5 %all_gather.7 = f32[8,64,192]{1,2,0:T(8,128)S(1)} all-gather(f32[8,64,24]{1,2,0:T(8,128)S(1)} %fusion.16), channel_id=1, replica_groups=mesh['box'=64,'row'=8] {'row'}, dimensions={2}, use_global_device_ids=true | all-gather | bytes 442368 | tf_op jit(solution)/shard_map/all_gather | solution.py:60
  71.0 5.9 %gather_fusion.2 = bf16[1152,64]{1,0:T(8,128)(2,1)S(1)} fusion(f32[1,64,1536]{1,2,0:T(8,128)S(1)} %bitcast.117, s32[1152]{0:T(1024)S(1)} %fusion.29), kind=kCustom, calls=%fused_computation.2 | custom fusion | bytes 304128 | tf_op jit(solution)/shard_map/vmap()/gather | solution.py:14
  77.2 0.3 fusion.19
  77.6 1.9 %collective-permute-start.4 = (f32[1,64,48]{1,2,0:T(8,128)S(1)}, f32[1,64,48]{1,2,0:T(8,128)S(1)}, u32[]{:S(2)}, u32[]{:S(2)}) collective-permute-start(f32[1,64,48]{1,2,0:T(8,128)S(1)} %bitcast.128), channel_id=1, source_target_pairs={{0,8},{8,16},{16,24},{24,32},{32,40},{40,48},{48,56},{56,64},{64,7... | collective-permute-start | bytes 36872 | tf_op jit(solution)/shard_map/ppermute | solution.py:10
  79.5 6.0 %collective-permute-start.5 = (f32[1,64,48]{1,2,0:T(8,128)S(1)}, f32[1,64,48]{1,2,0:T(8,128)S(1)}, u32[]{:S(2)}, u32[]{:S(2)}) collective-permute-start(f32[1,64,48]{1,2,0:T(8,128)S(1)} %bitcast.127), channel_id=1, source_target_pairs={{8,0},{16,8},{24,16},{32,24},{40,32},{48,40},{56,48},{64,56},{72,6... | collective-permute-start | bytes 36872 | tf_op jit(solution)/shard_map/ppermute | solution.py:10
  85.6 0.9 %convolution_bitcast_fusion.1 = f32[1,64,144]{2,1,0:T(8,128)} fusion(bf16[1,1152,144]{1,2,0:T(8,128)(2,1)S(1)} %copy-done.1, bf16[1152,64]{1,0:T(8,128)(2,1)S(1)} %gather_fusion.2), kind=kOutput, calls=%fused_computation.6 | convolution fusion | flops 21233664 | bytes 516096 | tf_op jit(solution)/shard_map/pkr,prq->pkq/dot_general | solution.py:68
  86.5 0.8 gather_fusion.3
  87.3 0.8 fusion.22
  (44 shorter events, 1.0 us)
Async XLA Ops:
  0.6 24.6 %copy-start = (bf16[8,8,128,24]{2,3,1,0:T(8,128)(2,1)S(1)}, bf16[8,8,128,24]{2,3,1,0:T(8,128)(2,1)}, u32[]{:S(2)}) copy-start(bf16[8,8,128,24]{2,3,1,0:T(8,128)(2,1)} %param.18) | copy-start | bytes 1179652
  4.4 6.9 %copy-start.5 = (bf16[8,128,16]{1,2,0:T(8,128)(2,1)S(1)}, bf16[8,128,16]{1,2,0:T(8,128)(2,1)}, u32[]{:S(2)}) copy-start(bf16[8,128,16]{1,2,0:T(8,128)(2,1)} %param.17) | copy-start | bytes 98308
  25.6 23.2 %copy-start.8 = (s32[1,2]{1,0:T(1,128)S(1)}, s32[1,2]{1,0:T(1,128)}, u32[]{:S(2)}) copy-start(s32[1,2]{1,0:T(1,128)} %param.25) | copy-start | bytes 28
  26.5 23.1 %copy-start.6 = (s32[1,1152]{1,0:T(1,128)S(1)}, s32[1,1152]{1,0:T(1,128)}, u32[]{:S(2)}) copy-start(s32[1,1152]{1,0:T(1,128)} %param.21) | copy-start | bytes 13828
  26.5 23.1 %copy-start.7 = (s32[8,192]{1,0:T(8,128)S(1)}, s32[8,192]{1,0:T(8,128)}, u32[]{:S(2)}) copy-start(s32[8,192]{1,0:T(8,128)} %param.14) | copy-start | bytes 18436
  26.6 25.5 %collective-permute-start.3 = (f32[8,64,24]{1,2,0:T(8,128)S(1)}, f32[8,64,24]{1,2,0:T(8,128)S(1)}, u32[]{:S(2)}, u32[]{:S(2)}) collective-permute-start(f32[8,64,24]{1,2,0:T(8,128)S(1)} %bitcast.123), channel_id=1, source_target_pairs={{16,0},{24,8},{32,16},{40,24},{48,32},{56,40},{64,48},{72,56},{80,... | collective-permute-start | bytes 147464 | tf_op jit(solution)/shard_map/ppermute | solution.py:10
  38.7 13.4 %collective-permute-start = (f32[8,64,24]{1,2,0:T(8,128)S(1)}, f32[8,64,24]{1,2,0:T(8,128)S(1)}, u32[]{:S(2)}, u32[]{:S(2)}) collective-permute-start(f32[8,64,24]{1,2,0:T(8,128)S(1)} %bitcast.124), channel_id=1, source_target_pairs={{0,8},{8,16},{16,24},{24,32},{32,40},{40,48},{48,56},{56,64},{64,7... | collective-permute-start | bytes 147464 | tf_op jit(solution)/shard_map/ppermute | solution.py:10
  41.6 10.4 %collective-permute-start.1 = (f32[8,64,24]{1,2,0:T(8,128)S(1)}, f32[8,64,24]{1,2,0:T(8,128)S(1)}, u32[]{:S(2)}, u32[]{:S(2)}) collective-permute-start(f32[8,64,24]{1,2,0:T(8,128)S(1)} %bitcast.125), channel_id=1, source_target_pairs={{8,0},{16,8},{24,16},{32,24},{40,32},{48,40},{56,48},{64,56},{72,6... | collective-permute-start | bytes 147464 | tf_op jit(solution)/shard_map/ppermute | solution.py:10
  46.7 10.6 %copy-start.4 = (bf16[8,128,24]{1,2,0:T(8,128)(2,1)S(1)}, bf16[8,128,24]{1,2,0:T(8,128)(2,1)}, u32[]{:S(2)}) copy-start(bf16[8,128,24]{1,2,0:T(8,128)(2,1)} %param.16) | copy-start | bytes 147460
  46.7 10.6 %collective-permute-start.2 = (f32[8,64,24]{1,2,0:T(8,128)S(1)}, f32[8,64,24]{1,2,0:T(8,128)S(1)}, u32[]{:S(2)}, u32[]{:S(2)}) collective-permute-start(f32[8,64,24]{1,2,0:T(8,128)S(1)} %bitcast.126), channel_id=1, source_target_pairs={{0,16},{8,24},{16,32},{24,40},{32,48},{40,56},{48,64},{56,72},{64,... | collective-permute-start | bytes 147464 | tf_op jit(solution)/shard_map/ppermute | solution.py:10
  57.5 19.5 %copy-start.2 = (bf16[1,2,1152,48]{2,3,1,0:T(8,128)(2,1)S(1)}, bf16[1,2,1152,48]{2,3,1,0:T(8,128)(2,1)}, u32[]{:S(2)}) copy-start(bf16[1,2,1152,48]{2,3,1,0:T(8,128)(2,1)} %param.24) | copy-start | bytes 663556
  71.0 14.6 %copy-start.1 = (bf16[1,1152,144]{1,2,0:T(8,128)(2,1)S(1)}, bf16[1,1152,144]{1,2,0:T(8,128)(2,1)}, u32[]{:S(2)}) copy-start(bf16[1,1152,144]{1,2,0:T(8,128)(2,1)} %param.23) | copy-start | bytes 995332
  76.9 10.4 %copy-start.3 = (bf16[1,1152,48]{1,2,0:T(8,128)(2,1)S(1)}, bf16[1,1152,48]{1,2,0:T(8,128)(2,1)}, u32[]{:S(2)}) copy-start(bf16[1,1152,48]{1,2,0:T(8,128)(2,1)} %param.22) | copy-start | bytes 331780
  77.6 9.7 %collective-permute-start.4 = (f32[1,64,48]{1,2,0:T(8,128)S(1)}, f32[1,64,48]{1,2,0:T(8,128)S(1)}, u32[]{:S(2)}, u32[]{:S(2)}) collective-permute-start(f32[1,64,48]{1,2,0:T(8,128)S(1)} %bitcast.128), channel_id=1, source_target_pairs={{0,8},{8,16},{16,24},{24,32},{32,40},{40,48},{48,56},{56,64},{64,7... | collective-permute-start | bytes 36872 | tf_op jit(solution)/shard_map/ppermute | solution.py:10
  79.5 7.8 %collective-permute-start.5 = (f32[1,64,48]{1,2,0:T(8,128)S(1)}, f32[1,64,48]{1,2,0:T(8,128)S(1)}, u32[]{:S(2)}, u32[]{:S(2)}) collective-permute-start(f32[1,64,48]{1,2,0:T(8,128)S(1)} %bitcast.127), channel_id=1, source_target_pairs={{8,0},{16,8},{24,16},{32,24},{40,32},{48,40},{56,48},{64,56},{72,6... | collective-permute-start | bytes 36872 | tf_op jit(solution)/shard_map/ppermute | solution.py:10
where the time goes:
time: 88.6 us; the launch traced here: 88.1 us
  starting transfers between devices  30 us (34%)
  blocking collectives  26.7 us (30%)
  local copies, waits for them, and re-layouts  17.7 us (20%)
  waiting for transfers between devices  5.19 us (6%)
  matrix products  4.45 us (5%)
  other arithmetic  3.13 us (4%)
  between operations  1.01 us (1%)
    ppermute x6, starting transfers between devices, shifted(): return lax.ppermute(block, axis, route)  30 us
    gather x7, local copies, waits for them, and re-layouts, pick(): return jax.vmap(lambda block, where: block[:, where])(values, index)  15.9 us
    all_gather x1, blocking collectives, shards(): gathered = lax.all_gather(ys1 + routed_one, 'row', axis=2, tiled=True)  13.5 us
    all_gather x1, blocking collectives, shards(): lax.all_gather(w_one, 'row', axis=2, tiled=True)  13.2 us
    ppermute x6, waiting for transfers between devices, shifted(): return lax.ppermute(block, axis, route)  5.19 us
  transfers between devices with their start and end apart: 6, of which 1 were waited for; matrix products, arithmetic and copies ran while one was open for 6% of the time, Pallas kernels for 0%

commit v1 on v0

v1 whole, which is shorter than its diff:
```python
import functools

import jax
import jax.numpy as jnp
from jax import lax
from jax.experimental import pallas as pl
from jax.experimental.pallas import tpu as pltpu
from jax.sharding import PartitionSpec as P

MESH = pl.DeviceIdType.MESH
F32 = jnp.float32
BF16 = jnp.bfloat16
NROW = 8
STEPS = (-2, 2, -1, 1)


def nt(a, b):
    return lax.dot_general(a, b, (((1,), (1,)), ((), ())), preferred_element_type=F32)


def nn(a, b):
    return jnp.dot(a, b, preferred_element_type=F32)


def place(p):
    box = jnp.floor((p + 0.5) * (1.0 / 192.0))
    rest = p - 192.0 * box
    owner = jnp.floor((rest + 0.5) * (1.0 / 24.0))
    half = jnp.where(box >= 4.0, 1.0, 0.0)
    return 768.0 * half + 96.0 * owner + 24.0 * (box - 4.0 * half) + (rest - 24.0 * owner)


def kernel(
    nbox,
    rhs, skel1, red1, interp1, inv1, couple1, near1, skel2, red2, interp2, inv2, panel2, near2,
    out_one, out_two, out_skel,
    v_rhs, v_skel1, v_red1, v_interp1, v_inv1, v_couple, v_near1, v_skel2, v_red2, v_w2, v_near2,
    rhs16, xr, wall, routed, ys, own, box_send, box_recv, parent, w2s, pair_send, pair_recv,
    one_buf, two_buf, skel_buf,
    load_sem, out_sem, a_send, a_recv, b_send, b_recv, c_send, c_recv, d_send, d_recv,
):
    q = lax.axis_index("box")
    r = lax.axis_index("row")

    loads = []
    for source, target in (
        (red1, v_red1), (rhs, v_rhs), (inv1, v_inv1), (skel1, v_skel1), (interp1, v_interp1),
        (near1, v_near1), (couple1, v_couple), (red2, v_red2), (skel2, v_skel2), (near2, v_near2),
        (panel2, v_w2.at[0:96]), (interp2, v_w2.at[96:144]), (inv2, v_w2.at[144:288]),
    ):
        copy = pltpu.make_async_copy(source, target, load_sem.at[len(loads)])
        copy.start()
        loads.append(copy)

    barrier = pltpu.get_barrier_semaphore()
    row_peers = [lax.rem(r + i, NROW) for i in range(1, NROW)]
    box_peers = [lax.rem(q + nbox + step, nbox) for step in STEPS]
    for peer in row_peers:
        pl.semaphore_signal(barrier, inc=1, device_id=(q, peer), device_id_type=MESH)
    for peer in box_peers:
        pl.semaphore_signal(barrier, inc=1, device_id=(peer, r), device_id_type=MESH)

    low = lax.broadcasted_iota(jnp.int32, (1, 128), 1) < 64

    loads[0].wait()
    loads[1].wait()
    loads[2].wait()
    dof = lax.broadcasted_iota(jnp.int32, (320, 128), 0)
    for b in range(4):
        for h in range(2):
            box = b + 4 * h
            onehot = jnp.where(dof == v_red1[box : box + 1, :], 1.0, 0.0).astype(BF16)
            values = v_rhs[box * 64 : box * 64 + 64, :].astype(BF16)
            rhs16[b, h * 64 : h * 64 + 64, :] = values
            xr[b, h * 64 : h * 64 + 64, :] = nn(values, onehot).astype(BF16)
        x = xr[b]
        first = nt(v_inv1[b], x)
        second = nt(v_inv1[b + 4], x)
        one_buf[b * 16 : b * 16 + 16, :] = first[:, 0:64]
        one_buf[b * 16 + 64 : b * 16 + 80, :] = pltpu.roll(second, 64, 1)[:, 0:64]
        wall[b, pl.ds(pl.multiple_of(r * 16, 16), 16), :] = jnp.where(low, first, second).astype(BF16)

    pl.semaphore_wait(barrier, NROW - 1 + len(STEPS))

    def gather_copy(buffer, index, i, send, recv):
        return pltpu.make_async_remote_copy(
            src_ref=buffer.at[index], dst_ref=buffer.at[index],
            send_sem=send.at[i - 1], recv_sem=recv.at[i - 1],
            device_id=(q, row_peers[i - 1]), device_id_type=MESH,
        )

    mine_a = (slice(None), pl.ds(pl.multiple_of(r * 16, 16), 16), slice(None))
    copies_a = [gather_copy(wall, mine_a, i, a_send, a_recv) for i in range(1, NROW)]
    for i in (4, 3, 5, 2, 6, 1, 7):
        copies_a[i - 1].start()

    out_copy_one = pltpu.make_async_copy(one_buf, out_one, out_sem.at[0])
    out_copy_one.start()

    loads[3].wait()
    loads[4].wait()
    dof_lane = lax.broadcasted_iota(jnp.int32, (24, 320), 1).astype(F32)
    pick = (
        lax.broadcasted_iota(jnp.int32, (24, 192), 1)
        == lax.broadcasted_iota(jnp.int32, (24, 192), 0) + r * 24
    )
    for b in range(4):
        parts = []
        for h in range(2):
            box = b + 4 * h
            names = v_skel1[box : box + 1, :].astype(F32)
            column = jnp.sum(jnp.where(pick, names, 0.0), axis=1, keepdims=True)
            onehot = jnp.where(dof_lane == column, 1.0, 0.0).astype(BF16)
            parts.append(nt(onehot, rhs16[b]) - nt(v_interp1[box], xr[b]))
        ys[b * 24 : b * 24 + 24, :] = jnp.where(low, parts[0], parts[1])

    loads[5].wait()
    loads[6].wait()
    names = v_near1[...]
    relative = jnp.where(names < 0, -64, names - 8 * (q - 2)).astype(F32) * 24.0
    lane = lax.broadcasted_iota(jnp.int32, (8, 192), 1).astype(F32)
    slot = jnp.floor((lane + 0.5) * (1.0 / 24.0))
    key = lane - 24.0 * slot
    for j in range(8):
        key = key + jnp.where(slot == float(j), relative[:, j : j + 1], 0.0)
    key = key.astype(jnp.int32)
    row_id = lax.broadcasted_iota(jnp.int32, (960, 192), 0)
    for box in range(8):
        h, b = box // 4, box % 4
        onehot = jnp.where(row_id == key[box : box + 1, :], 1.0, 0.0).astype(BF16)
        routed[h * 960 : h * 960 + 960, b * 128 : b * 128 + 128] = nn(onehot, v_couple[box]).astype(BF16)

    for copy in copies_a:
        copy.wait_recv()

    w = wall[...].reshape(512, 128)
    copies_b = []
    for n, step in enumerate(STEPS + (0,)):
        base = (step + 2) * 192
        top = nn(routed[base : base + 192, :], w)
        bottom = nn(routed[960 + base : 960 + base + 192, :], w)
        keep = jnp.where(low, top[0:96], bottom[96:192])
        turn = jnp.where(low, top[96:192], bottom[0:96])
        total = keep + pltpu.roll(turn, 64, 1)
        if step == 0:
            own[...] = total + ys[...]
        else:
            box_send[n] = total.astype(BF16)
            copy = pltpu.make_async_remote_copy(
                src_ref=box_send.at[n], dst_ref=box_recv.at[n],
                send_sem=b_send.at[n], recv_sem=b_recv.at[n],
                device_id=(box_peers[n], r), device_id_type=MESH,
            )
            copy.start()
            copies_b.append(copy)

    for copy in loads[7:]:
        copy.wait()
    spots = place(v_red2[...].astype(F32)).astype(jnp.int32)
    pick2 = (
        lax.broadcasted_iota(jnp.int32, (48, 384), 1)
        == lax.broadcasted_iota(jnp.int32, (48, 384), 0) + r * 48
    )
    mine = jnp.sum(jnp.where(pick2, place(v_skel2[...].astype(F32)), 0.0), axis=1, keepdims=True)
    valid = jnp.where(v_near2[...] >= 0, 1.0, 0.0)
    valid = (valid[:, 0:1], valid[:, 1:2])
    spot_row = lax.broadcasted_iota(jnp.int32, (256, 1152), 0)
    spot_lane = lax.broadcasted_iota(jnp.int32, (48, 256), 1)
    mine = mine.astype(jnp.int32)

    def scatter(i):
        h, j = i // 3, i % 3
        onehot = jnp.where(spot_row + i * 256 == spots, 1.0, 0.0).astype(BF16)
        moved = nt(v_w2[...], onehot)
        chosen = jnp.where(spot_lane + i * 256 == mine, 1.0, 0.0)
        lanes = slice(j * 256, j * 256 + 256)
        w2s[h * 288 : h * 288 + 48, lanes] = (moved[0:48] * valid[0]).astype(BF16)
        w2s[h * 288 + 48 : h * 288 + 96, lanes] = (moved[48:96] * valid[1]).astype(BF16)
        w2s[h * 288 + 96 : h * 288 + 144, lanes] = (chosen - moved[96:144]).astype(BF16)
        w2s[h * 288 + 144 : h * 288 + 288, lanes] = moved[144:288].astype(BF16)

    for i in range(3):
        scatter(i)

    for copy in copies_b:
        copy.wait_recv()
    z = own[...]
    for n in range(4):
        z = z + box_recv[n].astype(F32)
    rows = pl.ds(pl.multiple_of(r * 96, 16), 96)
    parent[rows, :] = z.astype(BF16)
    copies_c = [gather_copy(parent, (rows, slice(None)), i, c_send, c_recv) for i in range(1, NROW)]
    for i in (4, 3, 5, 2, 6, 1, 7):
        copies_c[i - 1].start()

    for i in range(3, 6):
        scatter(i)

    for copy in copies_c:
        copy.wait_recv()

    p = parent[...]
    pair = nn(w2s[0:96, :], p) + pltpu.roll(nn(w2s[288:384, :], p), 64, 1)
    pair_send[...] = pair.astype(BF16).reshape(2, 48, 128)
    copies_d = []
    for n, step in enumerate((-1, 1)):
        copy = pltpu.make_async_remote_copy(
            src_ref=pair_send.at[n], dst_ref=pair_recv.at[n],
            send_sem=d_send.at[n], recv_sem=d_recv.at[n],
            device_id=(lax.rem(q + nbox + step, nbox), r), device_id_type=MESH,
        )
        copy.start()
        copies_d.append(copy)

    skel = nn(w2s[96:144, :], p) + pltpu.roll(nn(w2s[384:432, :], p), 64, 1)

    def tn(a, b):
        return lax.dot_general(a, b, (((0,), (1,)), ((), ())), preferred_element_type=F32)

    two_buf[...] = tn(p, w2s[144:288, :])[0:64] + tn(p, w2s[432:576, :])[64:128]
    out_copy_two = pltpu.make_async_copy(two_buf, out_two, out_sem.at[1])
    out_copy_two.start()

    for copy in copies_d:
        copy.wait_recv()
    skel = skel + pair_recv[0].astype(F32) + pair_recv[1].astype(F32)
    skel_buf[...] = skel[:, 0:64]
    out_copy_skel = pltpu.make_async_copy(skel_buf, out_skel, out_sem.at[2])
    out_copy_skel.start()
    for copy in copies_a + copies_b + copies_c + copies_d:
        copy.wait_send()
    out_copy_one.wait()
    out_copy_two.wait()
    out_copy_skel.wait()


def shards(nbox, rhs, skel1, red1, interp1, inv1, couple1, near1, skel2, red2, interp2, inv2, panel2, near2):
    turned = lambda a: jnp.swapaxes(a, -1, -2)
    operands = (
        rhs.reshape(512, 320), skel1, red1, turned(interp1), turned(inv1),
        turned(couple1).reshape(8, 192, 128), near1, skel2, red2,
        turned(interp2).reshape(48, 1152), turned(inv2).reshape(144, 1152),
        turned(panel2).reshape(96, 1152), near2,
    )
    dma = pltpu.SemaphoreType.DMA
    one, two, skel = pl.pallas_call(
        functools.partial(kernel, nbox),
        out_shape=(
            jax.ShapeDtypeStruct((128, 64), F32),
            jax.ShapeDtypeStruct((64, 144), F32),
            jax.ShapeDtypeStruct((48, 64), F32),
        ),
        in_specs=[pl.BlockSpec(memory_space=pl.ANY)] * len(operands),
        out_specs=(pl.BlockSpec(memory_space=pl.ANY),) * 3,
        scratch_shapes=[
            pltpu.VMEM((512, 320), F32),
            pltpu.VMEM((8, 192), jnp.int32),
            pltpu.VMEM((8, 128), jnp.int32),
            pltpu.VMEM((8, 24, 128), BF16),
            pltpu.VMEM((8, 16, 128), BF16),
            pltpu.VMEM((8, 192, 128), BF16),
            pltpu.VMEM((8, 8), jnp.int32),
            pltpu.VMEM((1, 384), jnp.int32),
            pltpu.VMEM((1, 1152), jnp.int32),
            pltpu.VMEM((288, 1152), BF16),
            pltpu.VMEM((1, 2), jnp.int32),
            pltpu.VMEM((4, 128, 320), BF16),
            pltpu.VMEM((4, 128, 128), BF16),
            pltpu.VMEM((4, 128, 128), BF16),
            pltpu.VMEM((1920, 512), BF16),
            pltpu.VMEM((96, 128), F32),
            pltpu.VMEM((96, 128), F32),
            pltpu.VMEM((4, 96, 128), BF16),
            pltpu.VMEM((4, 96, 128), BF16),
            pltpu.VMEM((768, 128), BF16),
            pltpu.VMEM((576, 768), BF16),
            pltpu.VMEM((2, 48, 128), BF16),
            pltpu.VMEM((2, 48, 128), BF16),
            pltpu.VMEM((128, 64), F32),
            pltpu.VMEM((64, 144), F32),
            pltpu.VMEM((48, 64), F32),
            dma((13,)), dma((3,)),
            dma((7,)), dma((7,)), dma((4,)), dma((4,)), dma((7,)), dma((7,)), dma((2,)), dma((2,)),
        ],
        compiler_params=pltpu.CompilerParams(
            collective_id=0, has_side_effects=True, vmem_limit_bytes=60 << 20
        ),
        name="skeleton_step",
    )(*operands)
    return (
        jnp.swapaxes(one.reshape(8, 16, 64), 1, 2),
        two.reshape(1, 64, 144),
        jnp.swapaxes(skel.reshape(1, 48, 64), 1, 2),
    )


def solution(mesh):
    return jax.shard_map(
        functools.partial(shards, mesh.shape["box"]),
        mesh=mesh,
        in_specs=(
            P("box", None, None),
            P("box", None),
            P("box", None),
            P("box", None, "row"),
            P("box", None, "row"),
            P("box", None, None, "row"),
            P("box", None),
            P("box", None),
            P("box", None),
            P("box", None, "row"),
            P("box", None, "row"),
            P("box", None, None, "row"),
            P("box", None),
        ),
        out_specs=(P("box", None, "row"), P("box", None, "row"), P("box", None, "row")),
        check_vma=False,
    )
```

time: 88.6 us -> 37.2 us (0.42)
  the two profiles are of different devices: /device:TPU:24 before, /device:TPU:1 now
where the time goes in v1:
time: 37.2 us; the launch traced here: 37 us
  Pallas kernels  33.5 us (90%)
  local copies, waits for them, and re-layouts  2.85 us (8%)
  between operations  0.65 us (2%)
    pallas_call x1, Pallas kernels, shards(): pl.pallas_call(functools.partial(kernel, nbox), out_shape=(jax.ShapeDtype...  33.5 us
    unnamed x7, local copies, waits for them, and re-layouts  2.85 us

profile of v1, /device:TPU:1, one launch (start us, length us, event | category | flops | bytes accessed | tf_op | source)
XLA Modules:
  0.0 37.0 jit_solution(5386178212531913818)
XLA Ops:
  0.6 33.5 %skeleton_step.1 = (f32[128,64]{1,0:T(8,128)}, f32[64,144]{1,0:T(8,128)}, f32[48,64]{1,0:T(8,128)}) custom-call(f32[512,320]{1,0:T(8,128)} %bitcast.22, s32[8,192]{1,0:T(8,128)} %skel1.1, s32[8,128]{1,0:T(8,128)} %red1.1, bf16[8,24,128]{2,1,0:T(8,128)(2,1)} %bitcast.29, bf16[8,16,128]{2,1,0:T(8,128)(2,1)} %bitcast.30, bf16[8,192,128]{2,1,0:T(8,128)(2,1)} %bitcast.23, ...), custom_call_target="tpu_custom_call" | custom-call | tf_op jit(solution)/shard_map/skeleton_step/pallas_call | solution.py:246
  34.1 0.0 copy-start
  34.1 1.5 %copy.19 = f32[8,64,16]{1,2,0:T(8,128)} copy(f32[8,64,16]{1,2,0:T(8,128)} %bitcast.28) | data formatting | bytes 65536
  35.6 0.0 copy-done
  35.6 0.0 copy-start.1
  35.6 0.6 %copy.20 = f32[1,64,144]{2,1,0:T(8,128)} copy(f32[1,64,144]{2,1,0:T(8,128)S(1)} %bitcast.27) | data formatting | bytes 73728
  36.2 0.1 copy-done.1
  36.4 0.6 %copy.21 = f32[1,64,48]{1,2,0:T(8,128)} copy(f32[1,64,48]{1,2,0:T(8,128)S(1)} %bitcast.31) | data formatting | bytes 24576
Async XLA Ops:
  34.1 1.5 %copy-start = (f32[64,144]{1,0:T(8,128)S(1)}, f32[64,144]{1,0:T(8,128)}, u32[]{:S(2)}) copy-start(f32[64,144]{1,0:T(8,128)} %get-tuple-element.7) | copy-start | bytes 110596
  35.6 0.7 %copy-start.1 = (f32[48,64]{1,0:T(8,128)S(1)}, f32[48,64]{1,0:T(8,128)}, u32[]{:S(2)}) copy-start(f32[48,64]{1,0:T(8,128)} %get-tuple-element.8) | copy-start | bytes 36868

commit v2 on v1

--- a/solution.py
+++ b/solution.py
@@ -12,6 +12,7 @@
 BF16 = jnp.bfloat16
 NROW = 8
 STEPS = (-2, 2, -1, 1)
+SHAPES = ((128, 64), (64, 144), (48, 64))
 
 
 def nt(a, b):
@@ -20,6 +21,10 @@
 
 def nn(a, b):
     return jnp.dot(a, b, preferred_element_type=F32)
+
+
+def inside(q, nbox):
+    return jnp.logical_and(q >= 0, q < nbox)
 
 
 def place(p):
@@ -33,11 +38,10 @@
 def kernel(
     nbox,
     rhs, skel1, red1, interp1, inv1, couple1, near1, skel2, red2, interp2, inv2, panel2, near2,
-    out_one, out_two, out_skel,
+    one_buf, two_buf, skel_buf,
     v_rhs, v_skel1, v_red1, v_interp1, v_inv1, v_couple, v_near1, v_skel2, v_red2, v_w2, v_near2,
     rhs16, xr, wall, routed, ys, own, box_send, box_recv, parent, w2s, pair_send, pair_recv,
-    one_buf, two_buf, skel_buf,
-    load_sem, out_sem, a_send, a_recv, b_send, b_recv, c_send, c_recv, d_send, d_recv,
+    load_sem, a_send, a_recv, b_send, b_recv, c_send, c_recv, d_send, d_recv,
 ):
     q = lax.axis_index("box")
     r = lax.axis_index("row")
@@ -54,11 +58,26 @@
 
     barrier = pltpu.get_barrier_semaphore()
     row_peers = [lax.rem(r + i, NROW) for i in range(1, NROW)]
-    box_peers = [lax.rem(q + nbox + step, nbox) for step in STEPS]
+    box_peers = [q + step for step in STEPS]
     for peer in row_peers:
         pl.semaphore_signal(barrier, inc=1, device_id=(q, peer), device_id_type=MESH)
-    for peer in box_peers:
-        pl.semaphore_signal(barrier, inc=1, device_id=(peer, r), device_id_type=MESH)
+    for step, peer in zip(STEPS, box_peers):
+
+        @pl.when(inside(q + step, nbox))
+        def _():
+            pl.semaphore_signal(barrier, inc=1, device_id=(peer, r), device_id_type=MESH)
+
+    for n, step in enumerate(STEPS):
+
+        @pl.when(jnp.logical_not(inside(q - step, nbox)))
+        def _():
+            box_recv[n] = jnp.zeros(box_recv.shape[1:], BF16)
+
+    for n, step in enumerate((-1, 1)):
+
+        @pl.when(jnp.logical_not(inside(q - step, nbox)))
+        def _():
+            pair_recv[n] = jnp.zeros(pair_recv.shape[1:], BF16)
 
     low = lax.broadcasted_iota(jnp.int32, (1, 128), 1) < 64
 
@@ -80,7 +99,8 @@
         one_buf[b * 16 + 64 : b * 16 + 80, :] = pltpu.roll(second, 64, 1)[:, 0:64]
         wall[b, pl.ds(pl.multiple_of(r * 16, 16), 16), :] = jnp.where(low, first, second).astype(BF16)
 
-    pl.semaphore_wait(barrier, NROW - 1 + len(STEPS))
+    greeted = sum(inside(q + step, nbox).astype(jnp.int32) for step in STEPS)
+    pl.semaphore_wait(barrier, NROW - 1 + greeted)
 
     def gather_copy(buffer, index, i, send, recv):
         return pltpu.make_async_remote_copy(
@@ -93,9 +113,6 @@
     copies_a = [gather_copy(wall, mine_a, i, a_send, a_recv) for i in range(1, NROW)]
     for i in (4, 3, 5, 2, 6, 1, 7):
         copies_a[i - 1].start()
-
-    out_copy_one = pltpu.make_async_copy(one_buf, out_one, out_sem.at[0])
-    out_copy_one.start()
 
     loads[3].wait()
     loads[4].wait()
@@ -117,7 +134,17 @@
     loads[5].wait()
     loads[6].wait()
     names = v_near1[...]
-    relative = jnp.where(names < 0, -64, names - 8 * (q - 2)).astype(F32) * 24.0
+    relative = (names - 8 * (q - 2)).astype(F32)
+    group = jnp.floor(relative * 0.125)
+    child = relative - 8.0 * group
+    spot = jnp.where(group == 0.0, 0.0, 4.0)
+    for n, step in enumerate(STEPS):
+        spot = jnp.where(group == step + 2.0, float(n), spot)
+    half = jnp.floor(child * 0.25)
+    quarter = child - 4.0 * half
+    chunk = jnp.floor(quarter * 0.5)
+    relative = 480.0 * chunk + 96.0 * spot + 48.0 * half + 24.0 * (quarter - 2.0 * chunk)
+    relative = jnp.where(names < 0, -64.0, relative)
     lane = lax.broadcasted_iota(jnp.int32, (8, 192), 1).astype(F32)
     slot = jnp.floor((lane + 0.5) * (1.0 / 24.0))
     key = lane - 24.0 * slot
@@ -134,25 +161,39 @@
         copy.wait_recv()
 
     w = wall[...].reshape(512, 128)
-    copies_b = []
-    for n, step in enumerate(STEPS + (0,)):
-        base = (step + 2) * 192
-        top = nn(routed[base : base + 192, :], w)
-        bottom = nn(routed[960 + base : 960 + base + 192, :], w)
-        keep = jnp.where(low, top[0:96], bottom[96:192])
-        turn = jnp.where(low, top[96:192], bottom[0:96])
-        total = keep + pltpu.roll(turn, 64, 1)
-        if step == 0:
-            own[...] = total + ys[...]
-        else:
-            box_send[n] = total.astype(BF16)
-            copy = pltpu.make_async_remote_copy(
-                src_ref=box_send.at[n], dst_ref=box_recv.at[n],
-                send_sem=b_send.at[n], recv_sem=b_recv.at[n],
-                device_id=(box_peers[n], r), device_id_type=MESH,
-            )
-            copy.start()
-            copies_b.append(copy)
+
+    def updates(start, count):
+        top = nn(routed[start : start + 96 * count, :], w)
+        bottom = nn(routed[960 + start : 960 + start + 96 * count, :], w)
+        totals = []
+        for n in range(count):
+            a = slice(96 * n, 96 * n + 48)
+            b = slice(96 * n + 48, 96 * n + 96)
+            keep = jnp.where(low, top[a], bottom[b])
+            turn = jnp.where(low, top[b], bottom[a])
+            totals.append(keep + pltpu.roll(turn, 64, 1))
+        return totals
+
+    def box_copy(n, chunk):
+        part = pl.ds(chunk * 48, 48)
+        return pltpu.make_async_remote_copy(
+            src_ref=box_send.at[n, part], dst_ref=box_recv.at[n, part],
+            send_sem=b_send.at[chunk, n], recv_sem=b_recv.at[chunk, n],
+            device_id=(box_peers[n], r), device_id_type=MESH,
+        )
+
+    for chunk in range(2):
+        for n, total in enumerate(updates(480 * chunk, 4)):
+            box_send[n, chunk * 48 : chunk * 48 + 48, :] = total.astype(BF16)
+        for n, step in enumerate(STEPS):
+
+            @pl.when(inside(q + step, nbox))
+            def _():
+                box_copy(n, chunk).start()
+
+    for chunk in range(2):
+        part = slice(chunk * 48, chunk * 48 + 48)
+        own[part, :] = updates(480 * chunk + 384, 1)[0] + ys[part, :]
 
     for copy in loads[7:]:
         copy.wait()
@@ -182,16 +223,23 @@
     for i in range(3):
         scatter(i)
 
-    for copy in copies_b:
-        copy.wait_recv()
-    z = own[...]
-    for n in range(4):
-        z = z + box_recv[n].astype(F32)
-    rows = pl.ds(pl.multiple_of(r * 96, 16), 96)
-    parent[rows, :] = z.astype(BF16)
-    copies_c = [gather_copy(parent, (rows, slice(None)), i, c_send, c_recv) for i in range(1, NROW)]
-    for i in (4, 3, 5, 2, 6, 1, 7):
-        copies_c[i - 1].start()
+    copies_c = []
+    for chunk in range(2):
+        for n, step in enumerate(STEPS):
+
+            @pl.when(inside(q - step, nbox))
+            def _():
+                box_copy(n, chunk).wait_recv()
+
+        part = slice(chunk * 48, chunk * 48 + 48)
+        z = own[part, :]
+        for n in range(4):
+            z = z + box_recv[n, part, :].astype(F32)
+        rows = pl.ds(pl.multiple_of(r * 96 + chunk * 48, 16), 48)
+        parent[rows, :] = z.astype(BF16)
+        for i in (4, 3, 5, 2, 6, 1, 7):
+            copies_c.append(gather_copy(parent, (rows, slice(None)), i, c_send.at[chunk], c_recv.at[chunk]))
+            copies_c[-1].start()
 
     for i in range(3, 6):
         scatter(i)
@@ -202,15 +250,18 @@
     p = parent[...]
     pair = nn(w2s[0:96, :], p) + pltpu.roll(nn(w2s[288:384, :], p), 64, 1)
     pair_send[...] = pair.astype(BF16).reshape(2, 48, 128)
-    copies_d = []
-    for n, step in enumerate((-1, 1)):
-        copy = pltpu.make_async_remote_copy(
+    def pair_copy(n, step):
+        return pltpu.make_async_remote_copy(
             src_ref=pair_send.at[n], dst_ref=pair_recv.at[n],
             send_sem=d_send.at[n], recv_sem=d_recv.at[n],
-            device_id=(lax.rem(q + nbox + step, nbox), r), device_id_type=MESH,
+            device_id=(q + step, r), device_id_type=MESH,
         )
-        copy.start()
-        copies_d.append(copy)
+
+    for n, step in enumerate((-1, 1)):
+
+        @pl.when(inside(q + step, nbox))
+        def _():
+            pair_copy(n, step).start()
 
     skel = nn(w2s[96:144, :], p) + pltpu.roll(nn(w2s[384:432, :], p), 64, 1)
 
@@ -218,20 +269,41 @@
         return lax.dot_general(a, b, (((0,), (1,)), ((), ())), preferred_element_type=F32)
 
     two_buf[...] = tn(p, w2s[144:288, :])[0:64] + tn(p, w2s[432:576, :])[64:128]
-    out_copy_two = pltpu.make_async_copy(two_buf, out_two, out_sem.at[1])
-    out_copy_two.start()
-
-    for copy in copies_d:
-        copy.wait_recv()
+
+    for n, step in enumerate((-1, 1)):
+
+        @pl.when(inside(q - step, nbox))
+        def _():
+            pair_copy(n, step).wait_recv()
+
     skel = skel + pair_recv[0].astype(F32) + pair_recv[1].astype(F32)
     skel_buf[...] = skel[:, 0:64]
-    out_copy_skel = pltpu.make_async_copy(skel_buf, out_skel, out_sem.at[2])
-    out_copy_skel.start()
-    for copy in copies_a + copies_b + copies_c + copies_d:
+    for n, step in enumerate(STEPS):
+
+        @pl.when(inside(q + step, nbox))
+        def _():
+            box_copy(n, 0).wait_send()
+            box_copy(n, 1).wait_send()
+
+    for n, step in enumerate((-1, 1)):
+
+        @pl.when(inside(q + step, nbox))
+        def _():
+            pair_copy(n, step).wait_send()
+
+    for copy in copies_a + copies_c:
         copy.wait_send()
-    out_copy_one.wait()
-    out_copy_two.wait()
-    out_copy_skel.wait()
+
+
+def finish(one, two, skel, out_one, out_two, out_skel, sem):
+    copies = [
+        pltpu.make_async_copy(source, target, sem.at[n])
+        for n, (source, target) in enumerate(((one, out_one), (two, out_two), (skel, out_skel)))
+    ]
+    for copy in copies:
+        copy.start()
+    for copy in copies:
+        copy.wait()
 
 
 def shards(nbox, rhs, skel1, red1, interp1, inv1, couple1, near1, skel2, red2, interp2, inv2, panel2, near2):
@@ -245,13 +317,9 @@
     dma = pltpu.SemaphoreType.DMA
     one, two, skel = pl.pallas_call(
         functools.partial(kernel, nbox),
-        out_shape=(
-            jax.ShapeDtypeStruct((128, 64), F32),
-            jax.ShapeDtypeStruct((64, 144), F32),
-            jax.ShapeDtypeStruct((48, 64), F32),
-        ),
+        out_shape=tuple(pltpu.VMEM(shape, F32) for shape in SHAPES),
         in_specs=[pl.BlockSpec(memory_space=pl.ANY)] * len(operands),
-        out_specs=(pl.BlockSpec(memory_space=pl.ANY),) * 3,
+        out_specs=(pl.BlockSpec(memory_space=pltpu.VMEM),) * 3,
         scratch_shapes=[
             pltpu.VMEM((512, 320), F32),
             pltpu.VMEM((8, 192), jnp.int32),
@@ -276,17 +344,22 @@
             pltpu.VMEM((576, 768), BF16),
             pltpu.VMEM((2, 48, 128), BF16),
             pltpu.VMEM((2, 48, 128), BF16),
-            pltpu.VMEM((128, 64), F32),
-            pltpu.VMEM((64, 144), F32),
-            pltpu.VMEM((48, 64), F32),
-            dma((13,)), dma((3,)),
-            dma((7,)), dma((7,)), dma((4,)), dma((4,)), dma((7,)), dma((7,)), dma((2,)), dma((2,)),
+            dma((13,)),
+            dma((7,)), dma((7,)), dma((2, 4)), dma((2, 4)), dma((2, 7)), dma((2, 7)), dma((2,)), dma((2,)),
         ],
         compiler_params=pltpu.CompilerParams(
             collective_id=0, has_side_effects=True, vmem_limit_bytes=60 << 20
         ),
         name="skeleton_step",
     )(*operands)
+    one, two, skel = pl.pallas_call(
+        finish,
+        out_shape=tuple(jax.ShapeDtypeStruct(shape, F32) for shape in SHAPES),
+        in_specs=[pl.BlockSpec(memory_space=pltpu.VMEM)] * 3,
+        out_specs=(pl.BlockSpec(memory_space=pl.ANY),) * 3,
+        scratch_shapes=[dma((3,))],
+        name="write_results",
+    )(*(pltpu.with_memory_space_constraint(a, pltpu.VMEM) for a in (one, two, skel)))
     return (
         jnp.swapaxes(one.reshape(8, 16, 64), 1, 2),
         two.reshape(1, 64, 144),

time: 37.2 us -> 30.5 us (0.82)
  the two profiles are of different devices: /device:TPU:1 before, /device:TPU:24 now
where the time goes in v2:
time: 30.5 us; the launch traced here: 30.3 us
  Pallas kernels  29.7 us (97%)
  between operations  0.64 us (2%)
    pallas_call x1, Pallas kernels, shards(): pl.pallas_call(functools.partial(kernel, nbox), out_shape=tuple((pltpu.VM...  29 us
    pallas_call x1, Pallas kernels, shards(): pl.pallas_call(finish, out_shape=tuple((jax.ShapeDtypeStruct(shape, F32)...  0.68 us

profile of v2, /device:TPU:24, one launch (start us, length us, event | category | flops | bytes accessed | tf_op | source)
XLA Modules:
  0.0 30.3 jit_solution(752855133166515277)
XLA Ops:
  0.6 29.0 %skeleton_step.1 = (f32[128,64]{1,0:T(8,128)S(1)}, f32[64,144]{1,0:T(8,128)S(1)}, f32[48,64]{1,0:T(8,128)S(1)}) custom-call(f32[512,320]{1,0:T(8,128)} %bitcast.22, s32[8,192]{1,0:T(8,128)} %skel1.1, s32[8,128]{1,0:T(8,128)} %red1.1, bf16[8,24,128]{2,1,0:T(8,128)(2,1)} %bitcast.27, bf16[8,16,128]{2,1,0:T(8,128)(2,1)} %bitcast.28, ...), custom_call_target="tpu_custom_call" | custom-call | tf_op jit(solution)/shard_map/skeleton_step/pallas_call | solution.py:318
  29.6 0.7 %write_results.1 = (f32[128,64]{1,0:T(8,128)}, f32[64,144]{1,0:T(8,128)}, f32[48,64]{1,0:T(8,128)}) custom-call(f32[128,64]{1,0:T(8,128)S(1)} %get-tuple-element.9.one, f32[64,144]{1,0:T(8,128)S(1)} %get-tuple-element.10.two, f32[48,64]{1,0:T(8,128)S(1)} %get-tuple-element.11.skel), custom_call_target="tpu_custom_call" | custom-call | tf_op jit(solution)/shard_map/write_results/pallas_call | solution.py:355

commit v3 on v2

--- a/solution.py
+++ b/solution.py
@@ -27,12 +27,12 @@
     return jnp.logical_and(q >= 0, q < nbox)
 
 
-def place(p):
+def place(p, stride):
     box = jnp.floor((p + 0.5) * (1.0 / 192.0))
     rest = p - 192.0 * box
     owner = jnp.floor((rest + 0.5) * (1.0 / 24.0))
     half = jnp.where(box >= 4.0, 1.0, 0.0)
-    return 768.0 * half + 96.0 * owner + 24.0 * (box - 4.0 * half) + (rest - 24.0 * owner)
+    return stride * (8.0 * half + owner) + 24.0 * (box - 4.0 * half) + (rest - 24.0 * owner)
 
 
 def kernel(
@@ -42,6 +42,7 @@
     v_rhs, v_skel1, v_red1, v_interp1, v_inv1, v_couple, v_near1, v_skel2, v_red2, v_w2, v_near2,
     rhs16, xr, wall, routed, ys, own, box_send, box_recv, parent, w2s, pair_send, pair_recv,
     load_sem, a_send, a_recv, b_send, b_recv, c_send, c_recv, d_send, d_recv,
+    deal_send, deal_recv, w_send, w_recv, ready,
 ):
     q = lax.axis_index("box")
     r = lax.axis_index("row")
@@ -61,11 +62,11 @@
     box_peers = [q + step for step in STEPS]
     for peer in row_peers:
         pl.semaphore_signal(barrier, inc=1, device_id=(q, peer), device_id_type=MESH)
-    for step, peer in zip(STEPS, box_peers):
+    for n, step in enumerate((-1, 1)):
 
         @pl.when(inside(q + step, nbox))
         def _():
-            pl.semaphore_signal(barrier, inc=1, device_id=(peer, r), device_id_type=MESH)
+            pl.semaphore_signal(barrier, inc=1, device_id=(q + step, r), device_id_type=MESH)
 
     for n, step in enumerate(STEPS):
 
@@ -99,8 +100,14 @@
         one_buf[b * 16 + 64 : b * 16 + 80, :] = pltpu.roll(second, 64, 1)[:, 0:64]
         wall[b, pl.ds(pl.multiple_of(r * 16, 16), 16), :] = jnp.where(low, first, second).astype(BF16)
 
-    greeted = sum(inside(q + step, nbox).astype(jnp.int32) for step in STEPS)
+    greeted = sum(inside(q + step, nbox).astype(jnp.int32) for step in (-1, 1))
     pl.semaphore_wait(barrier, NROW - 1 + greeted)
+
+    for n, step in enumerate((-1, 1)):
+
+        @pl.when(inside(q + step, nbox))
+        def _():
+            pl.semaphore_signal(ready.at[n], inc=1, device_id=(q + step, r), device_id_type=MESH)
 
     def gather_copy(buffer, index, i, send, recv):
         return pltpu.make_async_remote_copy(
@@ -113,6 +120,31 @@
     copies_a = [gather_copy(wall, mine_a, i, a_send, a_recv) for i in range(1, NROW)]
     for i in (4, 3, 5, 2, 6, 1, 7):
         copies_a[i - 1].start()
+
+    for n in (7, 9, 10):
+        loads[n].wait()
+    spots = place(v_red2[...].astype(F32), 128.0).astype(jnp.int32)
+    spot_row = lax.broadcasted_iota(jnp.int32, (256, 1152), 0)
+    valid = jnp.where(v_near2[...] >= 0, 1.0, 0.0)
+    valid = (valid[:, 0:1], valid[:, 1:2])
+    for i in range(8):
+        onehot = jnp.where(spot_row + i * 256 == spots, 1.0, 0.0).astype(BF16)
+        moved = nt(v_w2[0:96, :], onehot)
+        for n in range(2):
+            d, h = (2 * i + n) % 8, i // 4
+            lanes = slice(n * 128, n * 128 + 128)
+            deal_send[d, h * 96 : h * 96 + 48, :] = (moved[0:48, lanes] * valid[0]).astype(BF16)
+            deal_send[d, h * 96 + 48 : h * 96 + 96, :] = (moved[48:96, lanes] * valid[1]).astype(BF16)
+    deal_recv[r] = deal_send[r]
+    copies_w = []
+    for i in (4, 3, 5, 2, 6, 1, 7):
+        copy = pltpu.make_async_remote_copy(
+            src_ref=deal_send.at[row_peers[i - 1]], dst_ref=deal_recv.at[r],
+            send_sem=w_send.at[i - 1], recv_sem=w_recv.at[i - 1],
+            device_id=(q, row_peers[i - 1]), device_id_type=MESH,
+        )
+        copy.start()
+        copies_w.append(copy)
 
     loads[3].wait()
     loads[4].wait()
@@ -182,6 +214,12 @@
             device_id=(box_peers[n], r), device_id_type=MESH,
         )
 
+    for n, step in enumerate((-1, 1)):
+
+        @pl.when(inside(q - step, nbox))
+        def _():
+            pl.semaphore_wait(ready.at[n], 1)
+
     for chunk in range(2):
         for n, total in enumerate(updates(480 * chunk, 4)):
             box_send[n, chunk * 48 : chunk * 48 + 48, :] = total.astype(BF16)
@@ -195,30 +233,25 @@
         part = slice(chunk * 48, chunk * 48 + 48)
         own[part, :] = updates(480 * chunk + 384, 1)[0] + ys[part, :]
 
-    for copy in loads[7:]:
-        copy.wait()
-    spots = place(v_red2[...].astype(F32)).astype(jnp.int32)
+    for n in (8, 11, 12):
+        loads[n].wait()
+    spots = place(v_red2[...].astype(F32), 96.0).astype(jnp.int32)
     pick2 = (
         lax.broadcasted_iota(jnp.int32, (48, 384), 1)
         == lax.broadcasted_iota(jnp.int32, (48, 384), 0) + r * 48
     )
-    mine = jnp.sum(jnp.where(pick2, place(v_skel2[...].astype(F32)), 0.0), axis=1, keepdims=True)
-    valid = jnp.where(v_near2[...] >= 0, 1.0, 0.0)
-    valid = (valid[:, 0:1], valid[:, 1:2])
-    spot_row = lax.broadcasted_iota(jnp.int32, (256, 1152), 0)
+    mine = jnp.sum(jnp.where(pick2, place(v_skel2[...].astype(F32), 96.0), 0.0), axis=1, keepdims=True)
     spot_lane = lax.broadcasted_iota(jnp.int32, (48, 256), 1)
     mine = mine.astype(jnp.int32)
 
     def scatter(i):
         h, j = i // 3, i % 3
         onehot = jnp.where(spot_row + i * 256 == spots, 1.0, 0.0).astype(BF16)
-        moved = nt(v_w2[...], onehot)
+        moved = nt(v_w2[96:288, :], onehot)
         chosen = jnp.where(spot_lane + i * 256 == mine, 1.0, 0.0)
         lanes = slice(j * 256, j * 256 + 256)
-        w2s[h * 288 : h * 288 + 48, lanes] = (moved[0:48] * valid[0]).astype(BF16)
-        w2s[h * 288 + 48 : h * 288 + 96, lanes] = (moved[48:96] * valid[1]).astype(BF16)
-        w2s[h * 288 + 96 : h * 288 + 144, lanes] = (chosen - moved[96:144]).astype(BF16)
-        w2s[h * 288 + 144 : h * 288 + 288, lanes] = moved[144:288].astype(BF16)
+        w2s[h * 192 : h * 192 + 48, lanes] = (chosen - moved[0:48]).astype(BF16)
+        w2s[h * 192 + 48 : h * 192 + 192, lanes] = moved[48:192].astype(BF16)
 
     for i in range(3):
         scatter(i)
@@ -241,6 +274,39 @@
             copies_c.append(gather_copy(parent, (rows, slice(None)), i, c_send.at[chunk], c_recv.at[chunk]))
             copies_c[-1].start()
 
+    for copy in copies_w:
+        copy.wait_recv()
+    block = parent[pl.ds(pl.multiple_of(r * 96, 16), 96), :]
+
+    def pair_copy(n, step, row):
+        return pltpu.make_async_remote_copy(
+            src_ref=pair_send.at[n, row], dst_ref=pair_recv.at[n, r],
+            send_sem=d_send.at[n, row], recv_sem=d_recv.at[n, r],
+            device_id=(q + step, row), device_id_type=MESH,
+        )
+
+    def pair_arrival(n, row):
+        return pltpu.make_async_remote_copy(
+            src_ref=pair_send.at[n, row], dst_ref=pair_recv.at[n, row],
+            send_sem=d_send.at[n, row], recv_sem=d_recv.at[n, row],
+            device_id=(q, row), device_id_type=MESH,
+        )
+
+    deal = nn(deal_recv[...].reshape(1536, 128)[:, 0:96], block)
+    for row in range(NROW):
+        for n in range(2):
+            a = row * 192 + n * 48
+            b = a + 96
+            keep = jnp.where(low, deal[a : a + 24], deal[b + 24 : b + 48])
+            turn = jnp.where(low, deal[a + 24 : a + 48], deal[b : b + 24])
+            pair_send[n, row] = (keep + pltpu.roll(turn, 64, 1)).astype(BF16)
+    for n, step in enumerate((-1, 1)):
+
+        @pl.when(inside(q + step, nbox))
+        def _():
+            for row in range(NROW):
+                pair_copy(n, step, row).start()
+
     for i in range(3, 6):
         scatter(i)
 
@@ -248,36 +314,23 @@
         copy.wait_recv()
 
     p = parent[...]
-    pair = nn(w2s[0:96, :], p) + pltpu.roll(nn(w2s[288:384, :], p), 64, 1)
-    pair_send[...] = pair.astype(BF16).reshape(2, 48, 128)
-    def pair_copy(n, step):
-        return pltpu.make_async_remote_copy(
-            src_ref=pair_send.at[n], dst_ref=pair_recv.at[n],
-            send_sem=d_send.at[n], recv_sem=d_recv.at[n],
-            device_id=(q + step, r), device_id_type=MESH,
-        )
-
-    for n, step in enumerate((-1, 1)):
-
-        @pl.when(inside(q + step, nbox))
-        def _():
-            pair_copy(n, step).start()
-
-    skel = nn(w2s[96:144, :], p) + pltpu.roll(nn(w2s[384:432, :], p), 64, 1)
+    skel = nn(w2s[0:48, :], p) + pltpu.roll(nn(w2s[192:240, :], p), 64, 1)
 
     def tn(a, b):
         return lax.dot_general(a, b, (((0,), (1,)), ((), ())), preferred_element_type=F32)
 
-    two_buf[...] = tn(p, w2s[144:288, :])[0:64] + tn(p, w2s[432:576, :])[64:128]
+    two_buf[...] = tn(p, w2s[48:192, :])[0:64] + tn(p, w2s[240:384, :])[64:128]
 
     for n, step in enumerate((-1, 1)):
 
         @pl.when(inside(q - step, nbox))
         def _():
-            pair_copy(n, step).wait_recv()
-
-    skel = skel + pair_recv[0].astype(F32) + pair_recv[1].astype(F32)
-    skel_buf[...] = skel[:, 0:64]
+            for row in range(NROW):
+                pair_arrival(n, row).wait_recv()
+
+    pairs = jnp.sum(pair_recv[...].astype(F32).reshape(16, 24, 128), axis=0)
+    skel_buf[0:24, :] = (skel[0:24] + pairs)[:, 0:64]
+    skel_buf[24:48, :] = (skel[24:48] + pltpu.roll(pairs, 64, 1))[:, 0:64]
     for n, step in enumerate(STEPS):
 
         @pl.when(inside(q + step, nbox))
@@ -289,9 +342,10 @@
 
         @pl.when(inside(q + step, nbox))
         def _():
-            pair_copy(n, step).wait_send()
-
-    for copy in copies_a + copies_c:
+            for row in range(NROW):
+                pair_copy(n, step, row).wait_send()
+
+    for copy in copies_a + copies_w + copies_c:
         copy.wait_send()
 
 
@@ -341,11 +395,14 @@
             pltpu.VMEM((4, 96, 128), BF16),
             pltpu.VMEM((4, 96, 128), BF16),
             pltpu.VMEM((768, 128), BF16),
-            pltpu.VMEM((576, 768), BF16),
-            pltpu.VMEM((2, 48, 128), BF16),
-            pltpu.VMEM((2, 48, 128), BF16),
+            pltpu.VMEM((384, 768), BF16),
+            pltpu.VMEM((2, NROW, 24, 128), BF16),
+            pltpu.VMEM((2, NROW, 24, 128), BF16),
             dma((13,)),
-            dma((7,)), dma((7,)), dma((2, 4)), dma((2, 4)), dma((2, 7)), dma((2, 7)), dma((2,)), dma((2,)),
+            dma((7,)), dma((7,)), dma((2, 4)), dma((2, 4)), dma((2, 7)), dma((2, 7)), dma((2, 8)), dma((2, 8)),
+            pltpu.VMEM((NROW, 192, 128), BF16),
+            pltpu.VMEM((NROW, 192, 128), BF16),
+            dma((7,)), dma((7,)), pltpu.SemaphoreType.REGULAR((2,)),
         ],
         compiler_params=pltpu.CompilerParams(
             collective_id=0, has_side_effects=True, vmem_limit_bytes=60 << 20

time: 30.5 us -> 29.1 us (0.954)
  Pallas kernels: 29.7 us -> 28.1 us
    pallas_call x1, Pallas kernels: 29 us -> 27.4 us  [shards(): pl.pallas_call(functools.partial(kernel, nbox), out_shape=tuple((pltpu.VM...]
where the time goes in v3:
time: 29.1 us; the launch traced here: 28.7 us
  Pallas kernels  28.1 us (97%)
  between operations  0.64 us (2%)
    pallas_call x1, Pallas kernels, shards(): pl.pallas_call(functools.partial(kernel, nbox), out_shape=tuple((pltpu.VM...  27.4 us
    pallas_call x1, Pallas kernels, shards(): pl.pallas_call(finish, out_shape=tuple((jax.ShapeDtypeStruct(shape, F32)...  0.68 us

profile of v3, /device:TPU:24, one launch (start us, length us, event | category | flops | bytes accessed | tf_op | source)
XLA Modules:
  0.0 28.7 jit_solution(12767675060250510019)
XLA Ops:
  0.6 27.4 %skeleton_step.1 = (f32[128,64]{1,0:T(8,128)S(1)}, f32[64,144]{1,0:T(8,128)S(1)}, f32[48,64]{1,0:T(8,128)S(1)}) custom-call(f32[512,320]{1,0:T(8,128)} %bitcast.22, s32[8,192]{1,0:T(8,128)} %skel1.1, s32[8,128]{1,0:T(8,128)} %red1.1, bf16[8,24,128]{2,1,0:T(8,128)(2,1)} %bitcast.27, bf16[8,16,128]{2,1,0:T(8,128)(2,1)} %bitcast.28, ...), custom_call_target="tpu_custom_call" | custom-call | tf_op jit(solution)/shard_map/skeleton_step/pallas_call | solution.py:372
  28.0 0.7 %write_results.1 = (f32[128,64]{1,0:T(8,128)}, f32[64,144]{1,0:T(8,128)}, f32[48,64]{1,0:T(8,128)}) custom-call(f32[128,64]{1,0:T(8,128)S(1)} %get-tuple-element.9.one, f32[64,144]{1,0:T(8,128)S(1)} %get-tuple-element.10.two, f32[48,64]{1,0:T(8,128)S(1)} %get-tuple-element.11.skel), custom_call_target="tpu_custom_call" | custom-call | tf_op jit(solution)/shard_map/write_results/pallas_call | solution.py:412

commit v4 on v3

--- a/solution.py
+++ b/solution.py
@@ -23,16 +23,26 @@
     return jnp.dot(a, b, preferred_element_type=F32)
 
 
+def one_hot(targets, start, rows, twice=None):
+    shift = targets - float(start)
+    shift = jnp.where(shift < float(rows), shift, -1.0).astype(BF16)
+    row = lax.broadcasted_iota(jnp.int32, (rows, targets.shape[1]), 0)
+    if twice is not None:
+        row = jnp.where(row < twice, row, row - (rows - twice))
+    row = row.astype(F32).astype(BF16)
+    return jnp.where(row == shift, jnp.ones((), BF16), jnp.zeros((), BF16))
+
+
 def inside(q, nbox):
     return jnp.logical_and(q >= 0, q < nbox)
 
 
-def place(p, stride):
+def place(p, stride, halves):
     box = jnp.floor((p + 0.5) * (1.0 / 192.0))
     rest = p - 192.0 * box
     owner = jnp.floor((rest + 0.5) * (1.0 / 24.0))
     half = jnp.where(box >= 4.0, 1.0, 0.0)
-    return stride * (8.0 * half + owner) + 24.0 * (box - 4.0 * half) + (rest - 24.0 * owner)
+    return stride * owner + halves * half + 24.0 * (box - 4.0 * half) + (rest - 24.0 * owner)
 
 
 def kernel(
@@ -42,7 +52,7 @@
     v_rhs, v_skel1, v_red1, v_interp1, v_inv1, v_couple, v_near1, v_skel2, v_red2, v_w2, v_near2,
     rhs16, xr, wall, routed, ys, own, box_send, box_recv, parent, w2s, pair_send, pair_recv,
     load_sem, a_send, a_recv, b_send, b_recv, c_send, c_recv, d_send, d_recv,
-    deal_send, deal_recv, w_send, w_recv, ready,
+    deal_send, deal_recv, deal_rest, w_send, w_recv, ready,
 ):
     q = lax.axis_index("box")
     r = lax.axis_index("row")
@@ -123,18 +133,17 @@
 
     for n in (7, 9, 10):
         loads[n].wait()
-    spots = place(v_red2[...].astype(F32), 128.0).astype(jnp.int32)
-    spot_row = lax.broadcasted_iota(jnp.int32, (256, 1152), 0)
+    spots = place(v_red2[...].astype(F32), 256.0, 96.0)
     valid = jnp.where(v_near2[...] >= 0, 1.0, 0.0)
     valid = (valid[:, 0:1], valid[:, 1:2])
-    for i in range(8):
-        onehot = jnp.where(spot_row + i * 256 == spots, 1.0, 0.0).astype(BF16)
-        moved = nt(v_w2[0:96, :], onehot)
+    for d in range(NROW):
+        moved = nt(v_w2[0:96, :], one_hot(spots, d * 256, 256, 192))
         for n in range(2):
-            d, h = (2 * i + n) % 8, i // 4
-            lanes = slice(n * 128, n * 128 + 128)
-            deal_send[d, h * 96 : h * 96 + 48, :] = (moved[0:48, lanes] * valid[0]).astype(BF16)
-            deal_send[d, h * 96 + 48 : h * 96 + 96, :] = (moved[48:96, lanes] * valid[1]).astype(BF16)
+            part = moved[n * 48 : n * 48 + 48] * valid[n]
+            deal_send[d, n * 48 : n * 48 + 48, :] = part[:, 0:128].astype(BF16)
+            rest = jnp.where(low, part[0:24, 128:256], part[24:48, 128:256])
+            deal_rest[d, n * 24 : n * 24 + 24, :] = rest
+        deal_send[d, 96:144, :] = deal_rest[d].astype(BF16)
     deal_recv[r] = deal_send[r]
     copies_w = []
     for i in (4, 3, 5, 2, 6, 1, 7):
@@ -182,12 +191,11 @@
     key = lane - 24.0 * slot
     for j in range(8):
         key = key + jnp.where(slot == float(j), relative[:, j : j + 1], 0.0)
-    key = key.astype(jnp.int32)
-    row_id = lax.broadcasted_iota(jnp.int32, (960, 192), 0)
     for box in range(8):
         h, b = box // 4, box % 4
-        onehot = jnp.where(row_id == key[box : box + 1, :], 1.0, 0.0).astype(BF16)
-        routed[h * 960 : h * 960 + 960, b * 128 : b * 128 + 128] = nn(onehot, v_couple[box]).astype(BF16)
+        for start in range(0, 960, 240):
+            moved = nn(one_hot(key[box : box + 1, :], start, 240), v_couple[box])
+            routed[h * 960 + start : h * 960 + start + 240, b * 128 : b * 128 + 128] = moved.astype(BF16)
 
     for copy in copies_a:
         copy.wait_recv()
@@ -235,19 +243,18 @@
 
     for n in (8, 11, 12):
         loads[n].wait()
-    spots = place(v_red2[...].astype(F32), 96.0).astype(jnp.int32)
+    spots = place(v_red2[...].astype(F32), 96.0, 768.0)
     pick2 = (
         lax.broadcasted_iota(jnp.int32, (48, 384), 1)
         == lax.broadcasted_iota(jnp.int32, (48, 384), 0) + r * 48
     )
-    mine = jnp.sum(jnp.where(pick2, place(v_skel2[...].astype(F32), 96.0), 0.0), axis=1, keepdims=True)
+    mine = jnp.sum(jnp.where(pick2, place(v_skel2[...].astype(F32), 96.0, 768.0), 0.0), axis=1, keepdims=True)
     spot_lane = lax.broadcasted_iota(jnp.int32, (48, 256), 1)
     mine = mine.astype(jnp.int32)
 
     def scatter(i):
         h, j = i // 3, i % 3
-        onehot = jnp.where(spot_row + i * 256 == spots, 1.0, 0.0).astype(BF16)
-        moved = nt(v_w2[96:288, :], onehot)
+        moved = nt(v_w2[96:288, :], one_hot(spots, i * 256, 256))
         chosen = jnp.where(spot_lane + i * 256 == mine, 1.0, 0.0)
         lanes = slice(j * 256, j * 256 + 256)
         w2s[h * 192 : h * 192 + 48, lanes] = (chosen - moved[0:48]).astype(BF16)
@@ -269,6 +276,7 @@
         for n in range(4):
             z = z + box_recv[n, part, :].astype(F32)
         rows = pl.ds(pl.multiple_of(r * 96 + chunk * 48, 16), 48)
+        own[part, :] = z
         parent[rows, :] = z.astype(BF16)
         for i in (4, 3, 5, 2, 6, 1, 7):
             copies_c.append(gather_copy(parent, (rows, slice(None)), i, c_send.at[chunk], c_recv.at[chunk]))
@@ -276,7 +284,13 @@
 
     for copy in copies_w:
         copy.wait_recv()
-    block = parent[pl.ds(pl.multiple_of(r * 96, 16), 96), :]
+    block = own[...]
+    turned = pltpu.roll(block, 64, 1)
+    lower = jnp.where(low, block, turned)
+    upper = jnp.where(low, turned, block)
+    first = jnp.concatenate([lower, upper[0:32]], axis=0).astype(BF16)
+    tail = upper[32:96]
+    second = jnp.concatenate([jnp.where(low, tail, 0.0), jnp.where(low, 0.0, tail)], axis=0).astype(BF16)
 
     def pair_copy(n, step, row):
         return pltpu.make_async_remote_copy(
@@ -292,14 +306,13 @@
             device_id=(q, row), device_id_type=MESH,
         )
 
-    deal = nn(deal_recv[...].reshape(1536, 128)[:, 0:96], block)
     for row in range(NROW):
+        main = nn(deal_recv[row, 0:96, :], first)
+        rest = nn(deal_recv[row, 96:144, :], second)
         for n in range(2):
-            a = row * 192 + n * 48
-            b = a + 96
-            keep = jnp.where(low, deal[a : a + 24], deal[b + 24 : b + 48])
-            turn = jnp.where(low, deal[a + 24 : a + 48], deal[b : b + 24])
-            pair_send[n, row] = (keep + pltpu.roll(turn, 64, 1)).astype(BF16)
+            a = n * 48
+            total = jnp.where(low, main[a : a + 24], main[a + 24 : a + 48]) + rest[n * 24 : n * 24 + 24]
+            pair_send[n, row] = total.astype(BF16)
     for n, step in enumerate((-1, 1)):
 
         @pl.when(inside(q + step, nbox))
@@ -400,8 +413,9 @@
             pltpu.VMEM((2, NROW, 24, 128), BF16),
             dma((13,)),
             dma((7,)), dma((7,)), dma((2, 4)), dma((2, 4)), dma((2, 7)), dma((2, 7)), dma((2, 8)), dma((2, 8)),
-            pltpu.VMEM((NROW, 192, 128), BF16),
-            pltpu.VMEM((NROW, 192, 128), BF16),
+            pltpu.VMEM((NROW, 144, 128), BF16),
+            pltpu.VMEM((NROW, 144, 128), BF16),
+            pltpu.VMEM((NROW, 48, 128), F32),
             dma((7,)), dma((7,)), pltpu.SemaphoreType.REGULAR((2,)),
         ],
         compiler_params=pltpu.CompilerParams(

time: 29.1 us -> 28.7 us (0.986)
  Pallas kernels: 28.1 us -> 27.6 us
    pallas_call x1, Pallas kernels: 27.4 us -> 26.9 us  [shards(): pl.pallas_call(functools.partial(kernel, nbox), out_shape=tuple((pltpu.VM...]
where the time goes in v4:
time: 28.7 us; the launch traced here: 28.3 us
  Pallas kernels  27.6 us (96%)
  between operations  0.64 us (2%)
    pallas_call x1, Pallas kernels, shards(): pl.pallas_call(functools.partial(kernel, nbox), out_shape=tuple((pltpu.VM...  26.9 us
    pallas_call x1, Pallas kernels, shards(): pl.pallas_call(finish, out_shape=tuple((jax.ShapeDtypeStruct(shape, F32)...  0.68 us

profile of v4, /device:TPU:24, one launch (start us, length us, event | category | flops | bytes accessed | tf_op | source)
XLA Modules:
  0.0 28.3 jit_solution(5755988577592197550)
XLA Ops:
  0.6 26.9 %skeleton_step.1 = (f32[128,64]{1,0:T(8,128)S(1)}, f32[64,144]{1,0:T(8,128)S(1)}, f32[48,64]{1,0:T(8,128)S(1)}) custom-call(f32[512,320]{1,0:T(8,128)} %bitcast.22, s32[8,192]{1,0:T(8,128)} %skel1.1, s32[8,128]{1,0:T(8,128)} %red1.1, bf16[8,24,128]{2,1,0:T(8,128)(2,1)} %bitcast.27, bf16[8,16,128]{2,1,0:T(8,128)(2,1)} %bitcast.28, ...), custom_call_target="tpu_custom_call" | custom-call | tf_op jit(solution)/shard_map/skeleton_step/pallas_call | solution.py:385
  27.6 0.7 %write_results.1 = (f32[128,64]{1,0:T(8,128)}, f32[64,144]{1,0:T(8,128)}, f32[48,64]{1,0:T(8,128)}) custom-call(f32[128,64]{1,0:T(8,128)S(1)} %get-tuple-element.9.one, f32[64,144]{1,0:T(8,128)S(1)} %get-tuple-element.10.two, f32[48,64]{1,0:T(8,128)S(1)} %get-tuple-element.11.skel), custom_call_target="tpu_custom_call" | custom-call | tf_op jit(solution)/shard_map/write_results/pallas_call | solution.py:426

commit v5 on v4

--- a/solution.py
+++ b/solution.py
@@ -130,6 +130,23 @@
     copies_a = [gather_copy(wall, mine_a, i, a_send, a_recv) for i in range(1, NROW)]
     for i in (4, 3, 5, 2, 6, 1, 7):
         copies_a[i - 1].start()
+
+    loads[3].wait()
+    loads[4].wait()
+    dof_lane = lax.broadcasted_iota(jnp.int32, (24, 320), 1).astype(F32)
+    pick = (
+        lax.broadcasted_iota(jnp.int32, (24, 192), 1)
+        == lax.broadcasted_iota(jnp.int32, (24, 192), 0) + r * 24
+    )
+    for b in range(4):
+        parts = []
+        for h in range(2):
+            box = b + 4 * h
+            names = v_skel1[box : box + 1, :].astype(F32)
+            column = jnp.sum(jnp.where(pick, names, 0.0), axis=1, keepdims=True)
+            onehot = jnp.where(dof_lane == column, 1.0, 0.0).astype(BF16)
+            parts.append(nt(onehot, rhs16[b]) - nt(v_interp1[box], xr[b]))
+        ys[b * 24 : b * 24 + 24, :] = jnp.where(low, parts[0], parts[1])
 
     for n in (7, 9, 10):
         loads[n].wait()
@@ -155,23 +172,6 @@
         copy.start()
         copies_w.append(copy)
 
-    loads[3].wait()
-    loads[4].wait()
-    dof_lane = lax.broadcasted_iota(jnp.int32, (24, 320), 1).astype(F32)
-    pick = (
-        lax.broadcasted_iota(jnp.int32, (24, 192), 1)
-        == lax.broadcasted_iota(jnp.int32, (24, 192), 0) + r * 24
-    )
-    for b in range(4):
-        parts = []
-        for h in range(2):
-            box = b + 4 * h
-            names = v_skel1[box : box + 1, :].astype(F32)
-            column = jnp.sum(jnp.where(pick, names, 0.0), axis=1, keepdims=True)
-            onehot = jnp.where(dof_lane == column, 1.0, 0.0).astype(BF16)
-            parts.append(nt(onehot, rhs16[b]) - nt(v_interp1[box], xr[b]))
-        ys[b * 24 : b * 24 + 24, :] = jnp.where(low, parts[0], parts[1])
-
     loads[5].wait()
     loads[6].wait()
     names = v_near1[...]
@@ -184,7 +184,9 @@
     half = jnp.floor(child * 0.25)
     quarter = child - 4.0 * half
     chunk = jnp.floor(quarter * 0.5)
-    relative = 480.0 * chunk + 96.0 * spot + 48.0 * half + 24.0 * (quarter - 2.0 * chunk)
+    ring = jnp.floor(spot * 0.5)
+    start = jnp.where(spot == 4.0, 768.0 + 96.0 * chunk, 384.0 * ring + 192.0 * chunk + 96.0 * (spot - 2.0 * ring))
+    relative = start + 48.0 * half + 24.0 * (quarter - 2.0 * chunk)
     relative = jnp.where(names < 0, -64.0, relative)
     lane = lax.broadcasted_iota(jnp.int32, (8, 192), 1).astype(F32)
     slot = jnp.floor((lane + 0.5) * (1.0 / 24.0))
@@ -228,18 +230,20 @@
         def _():
             pl.semaphore_wait(ready.at[n], 1)
 
-    for chunk in range(2):
-        for n, total in enumerate(updates(480 * chunk, 4)):
+    for ring in range(2):
+        for place_in, total in enumerate(updates(384 * ring, 4)):
+            chunk, n = place_in // 2, 2 * ring + place_in % 2
             box_send[n, chunk * 48 : chunk * 48 + 48, :] = total.astype(BF16)
-        for n, step in enumerate(STEPS):
-
-            @pl.when(inside(q + step, nbox))
-            def _():
-                box_copy(n, chunk).start()
-
-    for chunk in range(2):
+        for chunk in range(2):
+            for n in (2 * ring, 2 * ring + 1):
+
+                @pl.when(inside(q + STEPS[n], nbox))
+                def _():
+                    box_copy(n, chunk).start()
+
+    for chunk, total in enumerate(updates(768, 2)):
         part = slice(chunk * 48, chunk * 48 + 48)
-        own[part, :] = updates(480 * chunk + 384, 1)[0] + ys[part, :]
+        own[part, :] = total + ys[part, :]
 
     for n in (8, 11, 12):
         loads[n].wait()
@@ -280,7 +284,8 @@
         parent[rows, :] = z.astype(BF16)
         for i in (4, 3, 5, 2, 6, 1, 7):
             copies_c.append(gather_copy(parent, (rows, slice(None)), i, c_send.at[chunk], c_recv.at[chunk]))
-            copies_c[-1].start()
+            if chunk == 0:
+                copies_c[-1].start()
 
     for copy in copies_w:
         copy.wait_recv()
@@ -319,6 +324,9 @@
         def _():
             for row in range(NROW):
                 pair_copy(n, step, row).start()
+
+    for copy in copies_c[7:]:
+        copy.start()
 
     for i in range(3, 6):
         scatter(i)

time: 28.7 us -> 28.4 us (0.990)
  no operation moved by 1% of the time
where the time goes in v5:
time: 28.4 us; the launch traced here: 28 us
  Pallas kernels  27.4 us (96%)
  between operations  0.64 us (2%)
    pallas_call x1, Pallas kernels, shards(): pl.pallas_call(functools.partial(kernel, nbox), out_shape=tuple((pltpu.VM...  26.7 us
    pallas_call x1, Pallas kernels, shards(): pl.pallas_call(finish, out_shape=tuple((jax.ShapeDtypeStruct(shape, F32)...  0.68 us

profile of v5, /device:TPU:24, one launch (start us, length us, event | category | flops | bytes accessed | tf_op | source)
XLA Modules:
  0.0 28.0 jit_solution(3793415888207457305)
XLA Ops:
  0.6 26.7 %skeleton_step.1 = (f32[128,64]{1,0:T(8,128)S(1)}, f32[64,144]{1,0:T(8,128)S(1)}, f32[48,64]{1,0:T(8,128)S(1)}) custom-call(f32[512,320]{1,0:T(8,128)} %bitcast.22, s32[8,192]{1,0:T(8,128)} %skel1.1, s32[8,128]{1,0:T(8,128)} %red1.1, bf16[8,24,128]{2,1,0:T(8,128)(2,1)} %bitcast.27, bf16[8,16,128]{2,1,0:T(8,128)(2,1)} %bitcast.28, ...), custom_call_target="tpu_custom_call" | custom-call | tf_op jit(solution)/shard_map/skeleton_step/pallas_call | solution.py:393
  27.3 0.7 %write_results.1 = (f32[128,64]{1,0:T(8,128)}, f32[64,144]{1,0:T(8,128)}, f32[48,64]{1,0:T(8,128)}) custom-call(f32[128,64]{1,0:T(8,128)S(1)} %get-tuple-element.9.one, f32[64,144]{1,0:T(8,128)S(1)} %get-tuple-element.10.two, f32[48,64]{1,0:T(8,128)S(1)} %get-tuple-element.11.skel), custom_call_target="tpu_custom_call" | custom-call | tf_op jit(solution)/shard_map/write_results/pallas_call | solution.py:434

commit v6 on v5

--- a/solution.py
+++ b/solution.py
@@ -57,6 +57,17 @@
     q = lax.axis_index("box")
     r = lax.axis_index("row")
 
+    barrier = pltpu.get_barrier_semaphore()
+    row_peers = [lax.rem(r + i, NROW) for i in range(1, NROW)]
+    box_peers = [q + step for step in STEPS]
+    for i in (4, 3, 5, 2, 6, 1, 7):
+        pl.semaphore_signal(barrier, inc=1, device_id=(q, row_peers[i - 1]), device_id_type=MESH)
+    for n, step in enumerate((-1, 1)):
+
+        @pl.when(inside(q + step, nbox))
+        def _():
+            pl.semaphore_signal(barrier, inc=1, device_id=(q + step, r), device_id_type=MESH)
+
     loads = []
     for source, target in (
         (red1, v_red1), (rhs, v_rhs), (inv1, v_inv1), (skel1, v_skel1), (interp1, v_interp1),
@@ -66,17 +77,6 @@
         copy = pltpu.make_async_copy(source, target, load_sem.at[len(loads)])
         copy.start()
         loads.append(copy)
-
-    barrier = pltpu.get_barrier_semaphore()
-    row_peers = [lax.rem(r + i, NROW) for i in range(1, NROW)]
-    box_peers = [q + step for step in STEPS]
-    for peer in row_peers:
-        pl.semaphore_signal(barrier, inc=1, device_id=(q, peer), device_id_type=MESH)
-    for n, step in enumerate((-1, 1)):
-
-        @pl.when(inside(q + step, nbox))
-        def _():
-            pl.semaphore_signal(barrier, inc=1, device_id=(q + step, r), device_id_type=MESH)
 
     for n, step in enumerate(STEPS):
 

time: 28.4 us -> 28.3 us (level)
  no operation moved by 1% of the time
where the time goes in v6:
time: 28.3 us; the launch traced here: 28 us
  Pallas kernels  27.4 us (97%)
  between operations  0.64 us (2%)
    pallas_call x1, Pallas kernels, shards(): pl.pallas_call(functools.partial(kernel, nbox), out_shape=tuple((pltpu.VM...  26.7 us
    pallas_call x1, Pallas kernels, shards(): pl.pallas_call(finish, out_shape=tuple((jax.ShapeDtypeStruct(shape, F32)...  0.68 us

profile of v6, /device:TPU:24, one launch (start us, length us, event | category | flops | bytes accessed | tf_op | source)
XLA Modules:
  0.0 28.0 jit_solution(1715312211615021998)
XLA Ops:
  0.6 26.7 %skeleton_step.1 = (f32[128,64]{1,0:T(8,128)S(1)}, f32[64,144]{1,0:T(8,128)S(1)}, f32[48,64]{1,0:T(8,128)S(1)}) custom-call(f32[512,320]{1,0:T(8,128)} %bitcast.22, s32[8,192]{1,0:T(8,128)} %skel1.1, s32[8,128]{1,0:T(8,128)} %red1.1, bf16[8,24,128]{2,1,0:T(8,128)(2,1)} %bitcast.27, bf16[8,16,128]{2,1,0:T(8,128)(2,1)} %bitcast.28, ...), custom_call_target="tpu_custom_call" | custom-call | tf_op jit(solution)/shard_map/skeleton_step/pallas_call | solution.py:393
  27.3 0.7 %write_results.1 = (f32[128,64]{1,0:T(8,128)}, f32[64,144]{1,0:T(8,128)}, f32[48,64]{1,0:T(8,128)}) custom-call(f32[128,64]{1,0:T(8,128)S(1)} %get-tuple-element.9.one, f32[64,144]{1,0:T(8,128)S(1)} %get-tuple-element.10.two, f32[48,64]{1,0:T(8,128)S(1)} %get-tuple-element.11.skel), custom_call_target="tpu_custom_call" | custom-call | tf_op jit(solution)/shard_map/write_results/pallas_call | solution.py:434
